TPU v7x, 32 devices: a whole 2x2x4 slice. The times are simulated.
32 devices in a mesh: ctx: 4 (over z), rec: 8 (over y, x, core).
Axes of the slice: x: 2, y: 2, z: 4, core: 2. Of those that a mesh axis runs over, the one named last changes fastest.
Arguments:
- queries: bfloat16 [8, 1024, 1280], P('rec', 'ctx'), may hold values from -24 to 24
- video_keys: bfloat16 [8, 512, 1280], P('rec', 'ctx'), may hold values from -24 to 24
- video_values: bfloat16 [8, 512, 1280], P('rec', 'ctx'), may hold values from -6 to 6
- out_weight: bfloat16 [1280, 1280], replicated, may hold values from -0.15625 to 0.15625
- gate_logit: float32 [1], replicated, may hold values from 0.3 to 1.2
- row_grads: bfloat16 [16384, 1280], P(('ctx', 'rec')), may hold values from -6 to 6
- dest_device: int32 [16384], P(('ctx', 'rec')), may hold values from 0 to 31, as said below
- dest_row: int32 [16384], P(('ctx', 'rec')), may hold values from 0 to 255, as said below
- live_count: int32 [32], P(('ctx', 'rec')), may hold values from 0 to 512, as said below
Outputs:
- query_grads: bfloat16 [16384, 1280], P(('ctx', 'rec'))
- key_grads: bfloat16 [8, 512, 1280], P('rec', 'ctx')
- value_grads: bfloat16 [8, 512, 1280], P('rec', 'ctx')
- weight_grads: float32 [1280, 1280], P(('ctx', 'rec'))
- gate_grad: float32 [1], replicated
Inputs may be any that keep to these rules, and one draw needn't show every extreme that they name: `dest_device`: for the live slots of all devices together, each pair of owner device and audio row appears exactly once; the live slots of one device name one owner at most 16 times, and some device names each owner exactly 16 times. Slots that are not live hold 0. `dest_row`: slots that are not live hold 0. `live_count`: the live slots of a device are its first ones; the counts sum to 8192, and the largest is exactly 512.
All inputs are finite; a program needn't handle non-finite values.
Results may differ from a plain program's by a relative error of at most 0.012.
The roundings to bfloat16 on the way count: a program that leaves them out, or rounds other values in their place, can miss the bound.
Values may be sent and summed in bfloat16 or wider, within the bound.
No kernel may reach another device: no remote copies, remote signals or barrier semaphores. Data moves between devices by JAX's collectives and lax.ppermute only.
A program may use at most 192 MiB of HBM per device.

v0:
```python
import math
import jax
import jax.numpy as jnp
from jax import lax
from jax.sharding import PartitionSpec as P

HEADS = 20
HEAD_DIM = 64


def head_blocks(query_rows, keys_all, values_all, grad_attn):
    rows_q = query_rows.shape[0]
    rows_k = keys_all.shape[0]
    model_width = query_rows.shape[1]
    per_block = math.gcd(HEADS, 4)
    col_span = per_block * HEAD_DIM
    inv_root = HEAD_DIM ** (-0.5)
    attn_parts = []
    query_parts = []
    key_parts = []
    value_parts = []
    for block_idx in range(model_width // col_span):
        first_col = block_idx * col_span
        query_heads = query_rows[:, first_col : first_col + col_span].reshape(
            rows_q, per_block, HEAD_DIM
        )
        key_heads = keys_all[:, first_col : first_col + col_span].reshape(
            rows_k, per_block, HEAD_DIM
        )
        value_heads = values_all[:, first_col : first_col + col_span].reshape(
            rows_k, per_block, HEAD_DIM
        )
        grad_heads = grad_attn[:, first_col : first_col + col_span].reshape(
            rows_q, per_block, HEAD_DIM
        )
        scores = (
            jnp.einsum("ahd,vhd->hav", query_heads, key_heads, preferred_element_type=jnp.float32)
            * inv_root
        )
        row_peak = jnp.max(scores, axis=-1, keepdims=True)
        shifted = jnp.exp(scores - row_peak)
        softmax_w = shifted / jnp.sum(shifted, axis=-1, keepdims=True)
        probs_low = softmax_w.astype(jnp.bfloat16)
        attn_low = jnp.einsum(
            "hav,vhd->ahd", probs_low, value_heads, preferred_element_type=jnp.float32
        ).astype(jnp.bfloat16)
        row_delta = jnp.einsum(
            "ahd,ahd->ha", grad_heads, attn_low, preferred_element_type=jnp.float32
        )
        dprob = jnp.einsum(
            "ahd,vhd->hav", grad_heads, value_heads, preferred_element_type=jnp.float32
        )
        dscore = (softmax_w * (dprob - row_delta[:, :, None])).astype(jnp.bfloat16)
        query_part = (
            jnp.einsum("hav,vhd->ahd", dscore, key_heads, preferred_element_type=jnp.float32)
            * inv_root
        )
        key_part = (
            jnp.einsum("hav,ahd->vhd", dscore, query_heads, preferred_element_type=jnp.float32)
            * inv_root
        )
        value_part = jnp.einsum(
            "hav,ahd->vhd", probs_low, grad_heads, preferred_element_type=jnp.float32
        )
        attn_parts.append(attn_low.reshape(rows_q, col_span))
        query_parts.append(query_part.reshape(rows_q, col_span))
        key_parts.append(key_part.reshape(rows_k, col_span).astype(jnp.bfloat16))
        value_parts.append(value_part.reshape(rows_k, col_span).astype(jnp.bfloat16))
    return (
        jnp.concatenate(attn_parts, axis=1),
        jnp.concatenate(query_parts, axis=1),
        jnp.concatenate(key_parts, axis=1),
        jnp.concatenate(value_parts, axis=1),
    )


def local(
    queries,
    video_keys,
    video_values,
    out_weight,
    gate_logit,
    row_grads,
    dest_device,
    dest_row,
    live_count,
):
    ctx_count = lax.axis_size("ctx")
    rec_count = lax.axis_size("rec")
    all_count = ctx_count * rec_count
    slot_count = row_grads.shape[0]
    pair_cap = slot_count // all_count
    audio_rows = queries.shape[1]
    model_width = out_weight.shape[0]
    slot_ids = jnp.arange(slot_count, dtype=jnp.int32)
    is_live = slot_ids < live_count[0]
    owner_ids = jnp.arange(all_count, dtype=jnp.int32)
    owner_hot = jnp.logical_and(
        dest_device[:, None] == owner_ids[None, :], is_live[:, None]
    ).astype(jnp.bfloat16)
    earlier = (slot_ids[None, :] < slot_ids[:, None]).astype(jnp.bfloat16)
    before = jnp.dot(earlier, owner_hot, preferred_element_type=jnp.float32)
    bucket_rank = jnp.sum(before * owner_hot.astype(jnp.float32), axis=1).astype(jnp.int32)
    slot_target = jnp.where(is_live, dest_device * pair_cap + bucket_rank, slot_count)
    send_grads = (
        jnp.zeros((slot_count, model_width), jnp.bfloat16)
        .at[slot_target]
        .set(row_grads, mode="drop")
    )
    send_index = (
        jnp.full((slot_count,), audio_rows, jnp.int32).at[slot_target].set(dest_row, mode="drop")
    )
    recv_grads, recv_index = (
        lax.all_to_all(
            send_grads.reshape(all_count, pair_cap, model_width),
            ("ctx", "rec"),
            split_axis=0,
            concat_axis=0,
            tiled=True,
        ),
        lax.all_to_all(
            send_index.reshape(all_count, pair_cap),
            ("ctx", "rec"),
            split_axis=0,
            concat_axis=0,
            tiled=True,
        ),
    )
    recv_grads = recv_grads.reshape(slot_count, model_width)
    recv_index = recv_index.reshape(slot_count)
    grad_rows = (
        jnp.zeros((audio_rows + 1, model_width), jnp.bfloat16)
        .at[recv_index]
        .set(recv_grads)[:audio_rows]
    )
    keys_all, values_all = (
        lax.all_gather(video_keys, "ctx", axis=1, tiled=True),
        lax.all_gather(video_values, "ctx", axis=1, tiled=True),
    )
    gate_value = jnp.tanh(gate_logit[0])
    upstream = lax.dot_general(
        grad_rows, out_weight, (((1,), (1,)), ((), ())), preferred_element_type=jnp.float32
    )
    grad_attn = (gate_value * upstream).astype(jnp.bfloat16)
    attn_low, query_grad, key_term, value_term = head_blocks(
        queries[0], keys_all[0], values_all[0], grad_attn
    )
    key_sum, value_sum = (
        lax.psum_scatter(key_term[None], "ctx", scatter_dimension=1, tiled=True).astype(
            jnp.float32
        ),
        lax.psum_scatter(value_term[None], "ctx", scatter_dimension=1, tiled=True).astype(
            jnp.float32
        ),
    )
    weight_grad = lax.psum_scatter(
        gate_value
        * lax.dot_general(
            grad_rows, attn_low, (((0,), (0,)), ((), ())), preferred_element_type=jnp.float32
        ),
        ("ctx", "rec"),
        scatter_dimension=0,
        tiled=True,
    )
    shrink = 1.0 - gate_value * gate_value
    gate_total = lax.psum(jnp.sum(upstream * attn_low.astype(jnp.float32)), ("ctx", "rec"))
    gate_grad = shrink * gate_total
    padded_grad = jnp.concatenate(
        [query_grad.astype(jnp.bfloat16), jnp.zeros((1, model_width), jnp.bfloat16)], axis=0
    )
    back_rows = padded_grad[recv_index]
    returned = lax.all_to_all(
        back_rows.reshape(all_count, pair_cap, model_width),
        ("ctx", "rec"),
        split_axis=0,
        concat_axis=0,
        tiled=True,
    )
    returned = returned.reshape(slot_count, model_width)
    picked = returned[jnp.minimum(slot_target, slot_count - 1)]
    query_grads = jnp.where(is_live[:, None], picked, jnp.zeros((), jnp.bfloat16))
    return (
        query_grads,
        key_sum.astype(jnp.bfloat16),
        value_sum.astype(jnp.bfloat16),
        weight_grad,
        gate_grad.reshape(1),
    )


def solution(mesh):
    in_specs = (
        P("rec", "ctx", None),
        P("rec", "ctx", None),
        P("rec", "ctx", None),
        P(),
        P(),
        P(("ctx", "rec"), None),
        P(("ctx", "rec")),
        P(("ctx", "rec")),
        P(("ctx", "rec")),
    )
    out_specs = (
        P(("ctx", "rec"), None),
        P("rec", "ctx", None),
        P("rec", "ctx", None),
        P(("ctx", "rec"), None),
        P(),
    )
    return jax.shard_map(local, mesh=mesh, in_specs=in_specs, out_specs=out_specs, check_vma=False)
```

profile of v0, /device:TPU:0, one launch (start us, length us, event | category | flops | bytes accessed | tf_op | source)
XLA Modules:
  0.0 445.9 jit_solution(16039810445099604421)
XLA Ops:
  11.6 2.6 scatter_custom_fusion
  14.9 7.3 %all-to-all-start = ((s32[32,1,16]{2,1,0:T(1,128)}), s32[32,1,16]{2,1,0:T(1,128)S(1)}, u32[]{:S(2)}, u32[]{:S(2)}) async-start(s32[32,1,16]{2,1,0:T(1,128)} %bitcast.16), calls=%async_computation | async-start | bytes 32768 | tf_op jit(solution)/shard_map/all_to_all | solution.py:121
  22.2 1.9 fusion.67
  31.3 4.7 %scatter_custom_fusion.1 = bf16[512,1280]{1,0:T(8,128)(2,1)} fusion(s32[512]{0:T(512)} %copy-done.28, bf16[512,1280]{1,0:T(8,128)(2,1)} %param.14, bf16[]{:T(256)} %constant.14.clone.1), kind=kCustom, calls=%fused_computation.82 | custom fusion | bytes 1311232 | tf_op jit(solution)/shard_map/scatter | solution.py:108
  36.0 5.9 %all-to-all-start.1 = ((bf16[32,16,1280]{2,1,0:T(8,128)(2,1)}), bf16[32,16,1280]{2,1,0:T(8,128)(2,1)}, u32[]{:S(2)}, u32[]{:S(2)}) async-start(bf16[32,16,1280]{2,1,0:T(8,128)(2,1)} %bitcast.197), calls=%async_computation.1 | async-start | bytes 2621440 | tf_op jit(solution)/shard_map/all_to_all | solution.py:114
  43.5 2.0 all-gather.3.cloned.1.call-done
  45.5 2.2 fusion.65
  49.5 45.7 %all-gather.5.cloned.1.call-done = bf16[1,512,1280]{2,1,0:T(8,128)(2,1)} async-done(((bf16[1,128,1280]{2,1,0:T(8,128)(2,1)}), bf16[1,512,1280]{2,1,0:T(8,128)(2,1)}) %all-gather.5.cloned.1.call-update) | async-done | bytes 1310736 | tf_op jit(solution)/shard_map/all_gather | solution.py:138
  95.2 2.4 fusion.66
  104.7 1.8 copy.103
  106.5 1.8 copy.113
  110.1 1.8 copy.105
  112.8 3.2 fusion.69
  116.0 1.9 fusion.26
  120.0 3.1 fusion.70
  123.1 1.8 fusion.27
  127.2 3.2 fusion.71
  130.4 1.8 fusion.28
  135.9 3.8 fusion.72
  139.7 1.8 fusion.29
  145.3 3.8 fusion.73
  149.1 1.8 fusion.30
  162.7 4.3 scatter_custom_fusion.2
  167.0 3.0 multiply_reduce_fusion.5
  173.5 2.3 convolution_convert_fusion
  175.8 2.3 multiply_convert_fusion
  180.0 1.8 copy.129
  186.3 2.3 convolution_convert_fusion.1
  188.6 2.3 multiply_convert_fusion.1
  199.9 2.3 convolution_convert_fusion.2
  202.2 1.8 copy.132
  205.6 2.3 convolution_convert_fusion.3
  211.4 2.3 convolution_convert_fusion.4
  223.3 2.3 multiply_convert_fusion.2
  230.3 2.3 multiply_convert_fusion.3
  236.5 2.2 multiply_convert_fusion.4
  250.3 5.1 %convolution_multiply_fusion = f32[1280,1280]{1,0:T(8,128)} fusion(bf16[256,1280]{1,0:T(8,128)(2,1)} %constant_dynamic-update-slice_fusion.15, f32[]{:T(128)} %bitcast.15, bf16[257,1280]{1,0:T(8,128)(2,1)} %scatter_custom_fusion.2), kind=kOutput, calls=%fused_computation.10 | convolution fusion | flops 840499200 | bytes 7864832 | tf_op jit(solution)/shard_map/dot_general | solution.py:158
  256.3 2.3 fusion.19
  260.3 2.5 fusion.18
  264.5 2.4 fusion.17
  268.5 2.4 fusion.16
  272.5 2.3 fusion.15
  280.5 5.1 %gather_fusion = bf16[512,1280]{1,0:T(8,128)(2,1)} fusion(bf16[257,1280]{1,0:T(8,128)(2,1)} %concatenate.17, s32[1024]{0:T(1024)S(1)} %pad_clamp_fusion.1), kind=kCustom, calls=%fused_computation | custom fusion | bytes 2623488 | tf_op jit(solution)/shard_map/gather | solution.py:171
  285.6 3.8 all-to-all-start.2
  289.5 59.1 %psum.7 = f32[]{:T(128)} all-reduce(f32[]{:T(128)} %get-tuple-element.5), channel_id=1, replica_groups=mesh['ctx'=4,'rec'=8] {'ctx','rec'}, use_global_device_ids=true, to_apply=%region_18.19 | all-reduce | flops 1 | bytes 8 | tf_op jit(solution)/shard_map/psum | solution.py:166
  349.2 5.4 %gather_fusion.1 = bf16[512,1280]{1,0:T(8,128)(2,1)} fusion(bf16[512,1280]{1,0:T(8,128)(2,1)} %bitcast.70, s32[1024]{0:T(1024)S(1)} %pad_clamp_fusion), kind=kCustom, calls=%fused_computation.1 | custom fusion | bytes 2623488 | tf_op jit(solution)/shard_map/gather | solution.py:180
  354.7 2.5 broadcast_select_fusion
  357.2 81.1 %reduce-scatter.8.cloned.1.call-done = f32[40,1280]{1,0:T(8,128)} async-done(((f32[1280,1280]{1,0:T(8,128)}), f32[40,1280]{1,0:T(8,128)}) %reduce-scatter.8.cloned.1.call-update) | async-done | bytes 204816 | tf_op jit(solution)/shard_map/reduce_scatter | solution.py:156
  (159 shorter events, 114.5 us)
Async XLA Ops:
  7.2 159.8 %copy-start = (bf16[1280,1280]{1,0:T(8,128)(2,1)S(1)}, bf16[1280,1280]{1,0:T(8,128)(2,1)}, u32[]{:S(2)}) copy-start(bf16[1280,1280]{1,0:T(8,128)(2,1)} %param.12) | copy-start | bytes 9830404
  7.2 38.3 %all-gather.3.cloned.1.call-start = ((), (), s32[]{:S(2)}) async-start(), calls=%async_computation.6 | async-start | bytes 1638400 | tf_op jit(solution)/shard_map/all_gather | solution.py:137
  7.9 87.3 %all-gather.5.cloned.1.call-start = ((), (), s32[]{:S(2)}) async-start(), calls=%async_computation.7 | async-start | bytes 1638400 | tf_op jit(solution)/shard_map/all_gather | solution.py:138
  9.3 2.3 copy-start.29
  11.6 10.6 %copy-start.28 = (s32[512]{0:T(512)}, s32[512]{0:T(512)S(1)}, u32[]{:S(2)}) copy-start(s32[512]{0:T(512)S(1)} %get-tuple-element.28) | copy-start | bytes 6148
  14.9 21.1 %all-to-all-start = ((s32[32,1,16]{2,1,0:T(1,128)}), s32[32,1,16]{2,1,0:T(1,128)S(1)}, u32[]{:S(2)}, u32[]{:S(2)}) async-start(s32[32,1,16]{2,1,0:T(1,128)} %bitcast.16), calls=%async_computation | async-start | bytes 32768 | tf_op jit(solution)/shard_map/all_to_all | solution.py:121
  36.0 126.7 %all-to-all-start.1 = ((bf16[32,16,1280]{2,1,0:T(8,128)(2,1)}), bf16[32,16,1280]{2,1,0:T(8,128)(2,1)}, u32[]{:S(2)}, u32[]{:S(2)}) async-start(bf16[32,16,1280]{2,1,0:T(8,128)(2,1)} %bitcast.197), calls=%async_computation.1 | async-start | bytes 2621440 | tf_op jit(solution)/shard_map/all_to_all | solution.py:114
  41.9 315.2 %reduce-scatter.6.cloned.1.call-start = ((), (), s32[]{:S(2)}) async-start(), calls=%async_computation.9 | async-start | bytes 1638400 | tf_op jit(solution)/shard_map/reduce_scatter | solution.py:152
  116.0 2.9 copy-start.16
  116.0 4.1 copy-start.22
  117.8 1.0 copy-start.1
  123.1 2.9 copy-start.17
  125.0 1.0 copy-start.2
  130.4 2.8 copy-start.18
  132.2 1.0 copy-start.3
  139.7 2.8 copy-start.19
  141.6 1.0 copy-start.4
  149.1 2.8 copy-start.20
  151.0 1.0 copy-start.5
  175.8 3.3 copy-start.26
  178.1 1.0 copy-start.6
  188.6 3.4 copy-start.25
  190.9 1.1 copy-start.7
  215.5 7.0 %copy-start.13 = (bf16[512,256]{1,0:T(8,128)(2,1)S(1)}, bf16[512,256]{1,0:T(8,128)(2,1)}, u32[]{:S(2)}) copy-start(bf16[512,256]{1,0:T(8,128)(2,1)} %copy.134) | copy-start | bytes 786436
  223.2 134.0 %reduce-scatter.4.cloned.1.call-start = ((), (), s32[]{:S(2)}) async-start(), calls=%async_computation.8 | async-start | bytes 1638400 | tf_op jit(solution)/shard_map/reduce_scatter | solution.py:149
  223.3 3.3 copy-start.24
  225.6 1.0 copy-start.8
  230.3 3.4 copy-start.23
  230.3 6.2 %copy-start.11 = (bf16[256,256]{0,1:T(8,128)(2,1)S(1)}, bf16[256,256]{0,1:T(8,128)(2,1)}, u32[]{:S(2)}) copy-start(bf16[256,256]{0,1:T(8,128)(2,1)} %copy.102) | copy-start | bytes 393220
  232.6 1.1 copy-start.9
  236.5 3.2 copy-start.21
  238.7 1.0 copy-start.10
  239.7 9.7 %copy-start.12 = (bf16[512,256]{1,0:T(8,128)(2,1)S(1)}, bf16[512,256]{1,0:T(8,128)(2,1)}, u32[]{:S(2)}) copy-start(bf16[512,256]{1,0:T(8,128)(2,1)} %copy.129) | copy-start | bytes 786436
  250.2 188.1 %reduce-scatter.8.cloned.1.call-start = ((), (), s32[]{:S(2)}) async-start(), calls=%async_computation.10 | async-start | bytes 6758400 | tf_op jit(solution)/shard_map/reduce_scatter | solution.py:156
  255.3 0.9 copy-start.14
  262.8 9.7 %copy-start.15 = (bf16[512,256]{0,1:T(8,128)(2,1)S(1)}, bf16[512,256]{0,1:T(8,128)(2,1)}, u32[]{:S(2)}) copy-start(bf16[512,256]{0,1:T(8,128)(2,1)} %copy.100) | copy-start | bytes 786436
  285.6 3.9 copy-start.27
  285.6 63.6 %all-to-all-start.2 = ((bf16[32,16,1280]{2,1,0:T(8,128)(2,1)}), bf16[32,16,1280]{2,1,0:T(8,128)(2,1)}, u32[]{:S(2)}, u32[]{:S(2)}) async-start(bf16[32,16,1280]{2,1,0:T(8,128)(2,1)} %bitcast.196), calls=%async_computation.2 | async-start | bytes 2621440 | tf_op jit(solution)/shard_map/all_to_all | solution.py:172
  349.2 5.4 %copy-start.30 = (pred[512]{0:T(512)(128)(4,1)S(1)}, pred[512]{0:T(512)(128)(4,1)}, u32[]{:S(2)}) copy-start(pred[512]{0:T(512)(128)(4,1)} %copy-done.29) | copy-start | bytes 1540
Sparse Core Ops, SparseCore 0:
  9.6 35.8 all-gather.2
  47.0 48.1 all-gather.4
  223.3 30.4 reduce-scatter.5
  256.5 29.9 reduce-scatter.3
  289.3 148.9 reduce-scatter.7
where the time goes:
time: 449 us; the launch traced here: 446 us
  local copies, waits for them, and re-layouts  134 us (30%)
  waiting for transfers between devices  130 us (29%)
  matrix products  70 us (16%)
  blocking collectives  59.1 us (13%)
  other arithmetic  18.4 us (4%)
  starting transfers between devices  17.5 us (4%)
  between operations  17.3 us (4%)
    reduce_scatter x1, waiting for transfers between devices, local(): lax.psum_scatter(gate_value * lax.dot_general(grad_rows, attn_low, (((0,)...  81.1 us
    psum x1, blocking collectives, local(): lax.psum(jnp.sum(upstream * attn_low.astype(jnp.float32)), ('ctx', 'rec'))  59.1 us
    all_gather x1, waiting for transfers between devices, local(): lax.all_gather(video_values, 'ctx', axis=1, tiled=True)  45.7 us
    unnamed x78, local copies, waits for them, and re-layouts  33.9 us
    sub x5, matrix products, head_blocks(): shifted = jnp.exp(scores - row_peak)  17 us
    dot_general x5, matrix products, head_blocks(): jnp.einsum('hav,vhd->ahd', dscore, key_heads, preferred_element_type=jnp....  11.9 us
    dot_general x5, matrix products, head_blocks(): jnp.einsum('hav,ahd->vhd', probs_low, grad_heads, preferred_element_type=...  11.5 us
    dot_general x5, matrix products, head_blocks(): jnp.einsum('ahd,vhd->hav', grad_heads, value_heads, preferred_element_typ...  11.4 us
  transfers between devices with their start and end apart: 8, of which 3 were waited for; matrix products, arithmetic and copies ran while one was open for 34% of the time, Pallas kernels for 0%

commit v1 on v0

--- a/solution.py
+++ b/solution.py
@@ -6,6 +6,19 @@
 
 HEADS = 20
 HEAD_DIM = 64
+
+
+def collect(x, axis, dim):
+    ways = lax.axis_size(axis)
+    up = [(d, (d + 1) % ways) for d in range(ways)]
+    down = [(d, (d - 1) % ways) for d in range(ways)]
+    earlier, later = ([x], [x])
+    for _ in range(ways // 2):
+        earlier.append(lax.ppermute(earlier[-1], axis, up))
+    for _ in range((ways - 1) // 2):
+        later.append(lax.ppermute(later[-1], axis, down))
+    line = jnp.concatenate([*earlier[::-1], *later[1:]], axis=dim)
+    return jnp.roll(line, (lax.axis_index(axis) - ways // 2) * x.shape[dim], axis=dim)
 
 
 def head_blocks(query_rows, keys_all, values_all, grad_attn):
@@ -135,7 +148,7 @@
     )
     keys_all, values_all = (
         lax.all_gather(video_keys, "ctx", axis=1, tiled=True),
-        lax.all_gather(video_values, "ctx", axis=1, tiled=True),
+        collect(video_values, "ctx", 1),
     )
     gate_value = jnp.tanh(gate_logit[0])
     upstream = lax.dot_general(

time: 449 us -> 376 us (0.84)
  waiting for transfers between devices: 130 us -> 96.1 us
  local copies, waits for them, and re-layouts: 134 us -> 106 us
  matrix products: 70 us -> 54.3 us
  starting transfers between devices: 17.5 us -> 22.8 us
    all_gather x1 -> x0, waiting for transfers between devices: 45.7 us -> none  [local(): lax.all_gather(video_values, 'ctx', axis=1, tiled=True)]
    reduce_scatter x1, waiting for transfers between devices: 81.1 us -> 91.2 us  [local(): lax.psum_scatter(gate_value * lax.dot_general(grad_rows, attn_low, (((0,)...]
    ppermute x0 -> x3, starting transfers between devices: none -> 6.99 us  [the longest x2 4.9 us: collect(): earlier.append(lax.ppermute(earlier[-1], axis, up))]
    dot_general x5, matrix products: 11.5 us -> 4.58 us  [head_blocks(): jnp.einsum('hav,ahd->vhd', probs_low, grad_heads, preferred_element_type=...]
    slice x6, local copies, waits for them, and re-layouts: 9.11 us -> 3.95 us  [head_blocks(): grad_attn[:, first_col:first_col + col_span]]
    convert_element_type x5, local copies, waits for them, and re-layouts: 8.96 us -> 4.36 us  [head_blocks(): value_part.reshape(rows_k, col_span).astype(jnp.bfloat16)]
    unnamed x78 -> x121, local copies, waits for them, and re-layouts: 33.9 us -> 29.5 us
  transfers between devices with their start and end apart: 8 -> 10, of which waited for: 3 -> 3; matrix products, arithmetic and copies ran while one was open for 34% -> 38% of each run, Pallas kernels for 0% -> 0%
where the time goes in v1:
time: 376 us; the launch traced here: 374 us
  local copies, waits for them, and re-layouts  106 us (28%)
  waiting for transfers between devices  96.1 us (26%)
  blocking collectives  58.4 us (16%)
  matrix products  54.3 us (14%)
  starting transfers between devices  22.8 us (6%)
  other arithmetic  18.7 us (5%)
  between operations  17.7 us (5%)
    reduce_scatter x1, waiting for transfers between devices, local(): lax.psum_scatter(gate_value * lax.dot_general(grad_rows, attn_low, (((0,)...  91.2 us
    psum x1, blocking collectives, local(): lax.psum(jnp.sum(upstream * attn_low.astype(jnp.float32)), ('ctx', 'rec'))  58.4 us
    unnamed x121, local copies, waits for them, and re-layouts  29.5 us
    sub x5, matrix products, head_blocks(): shifted = jnp.exp(scores - row_peak)  15.6 us
    dot_general x5, matrix products, head_blocks(): jnp.einsum('ahd,vhd->hav', grad_heads, value_heads, preferred_element_typ...  10.5 us
    slice x6, local copies, waits for them, and re-layouts, head_blocks(): keys_all[:, first_col:first_col + col_span]  10.3 us
    convert_element_type x5, other arithmetic, head_blocks(): probs_low = softmax_w.astype(jnp.bfloat16)  9.24 us
    slice x6, local copies, waits for them, and re-layouts, head_blocks(): values_all[:, first_col:first_col + col_span]  9.01 us
  transfers between devices with their start and end apart: 10, of which 3 were waited for; matrix products, arithmetic and copies ran while one was open for 38% of the time, Pallas kernels for 0%

profile of v1, /device:TPU:0, one launch (start us, length us, event | category | flops | bytes accessed | tf_op | source)
XLA Modules:
  0.0 373.9 jit_solution(13959999925589503330)
XLA Ops:
  7.2 3.1 collective-permute-start
  10.3 2.1 collective-permute-start.2
  15.4 2.6 scatter_custom_fusion
  18.7 4.2 %all-to-all-start = ((s32[32,1,16]{2,1,0:T(1,128)}), s32[32,1,16]{2,1,0:T(1,128)S(1)}, u32[]{:S(2)}, u32[]{:S(2)}) async-start(s32[32,1,16]{2,1,0:T(1,128)} %bitcast.16), calls=%async_computation | async-start | bytes 32768 | tf_op jit(solution)/shard_map/all_to_all | solution.py:134
  22.9 1.8 collective-permute-start.1
  24.7 1.9 fusion.67
  33.8 4.7 %scatter_custom_fusion.1 = bf16[512,1280]{1,0:T(8,128)(2,1)} fusion(s32[512]{0:T(512)} %copy-done.46, bf16[512,1280]{1,0:T(8,128)(2,1)} %param.14, bf16[]{:T(256)} %constant.19.clone.1), kind=kCustom, calls=%fused_computation.83 | custom fusion | bytes 1311232 | tf_op jit(solution)/shard_map/scatter | solution.py:121
  38.5 4.2 %all-to-all-done = s32[32,1,16]{2,1,0:T(1,128)S(1)} async-done(((s32[32,1,16]{2,1,0:T(1,128)}), s32[32,1,16]{2,1,0:T(1,128)S(1)}, u32[]{:S(2)}, u32[]{:S(2)}) %all-to-all-start) | async-done | bytes 2080 | tf_op jit(solution)/shard_map/all_to_all | solution.py:134
  42.7 3.4 all-to-all-start.1
  55.8 1.8 copy.102
  57.6 1.8 copy.98
  59.4 1.8 copy.106
  61.2 1.8 copy.110
  64.6 2.3 fusion.65
  67.7 3.2 fusion.70
  70.9 1.9 fusion.27
  75.0 1.8 copy.95
  76.8 3.1 fusion.69
  79.9 1.9 fusion.26
  83.9 1.8 copy.104
  85.7 3.1 fusion.71
  88.9 1.9 fusion.28
  94.8 3.1 fusion.72
  97.8 1.8 fusion.29
  101.9 1.8 copy.112
  103.7 3.2 fusion.73
  106.9 1.8 fusion.30
  118.9 4.3 %scatter_custom_fusion.2 = bf16[257,1280]{1,0:T(8,128)(2,1)} fusion(s32[512]{0:T(512)S(1)} %bitcast.263, bf16[512,1280]{1,0:T(8,128)(2,1)} %bitcast.19, bf16[]{:T(256)} %constant.19.clone.1), kind=kCustom, calls=%fused_computation.88 | custom fusion | bytes 658432 | tf_op jit(solution)/shard_map/scatter | solution.py:147
  123.2 3.1 multiply_reduce_fusion.5
  130.8 2.0 convolution_convert_fusion.3
  132.8 1.8 copy.126
  150.0 2.2 multiply_convert_fusion.4
  153.4 2.3 multiply_convert_fusion.2
  156.7 1.8 copy.122
  159.5 2.3 multiply_convert_fusion.1
  163.8 1.8 copy.123
  165.6 2.2 multiply_convert_fusion
  169.8 1.8 copy.124
  178.4 5.1 %convolution_multiply_fusion = f32[1280,1280]{1,0:T(8,128)} fusion(bf16[256,1280]{1,0:T(8,128)(2,1)} %constant_dynamic-update-slice_fusion.23, f32[]{:T(128)} %bitcast.15, bf16[257,1280]{1,0:T(8,128)(2,1)} %scatter_custom_fusion.2), kind=kOutput, calls=%fused_computation.10 | convolution fusion | flops 840499200 | bytes 7864832 | tf_op jit(solution)/shard_map/dot_general | solution.py:171
  184.4 2.3 fusion.19
  187.8 2.4 fusion.18
  191.8 2.0 fusion.17
  197.1 2.9 gather_fusion
  199.9 7.8 %all-to-all-start.2 = ((bf16[32,16,1280]{2,1,0:T(8,128)(2,1)}), bf16[32,16,1280]{2,1,0:T(8,128)(2,1)}, u32[]{:S(2)}, u32[]{:S(2)}) async-start(bf16[32,16,1280]{2,1,0:T(8,128)(2,1)} %bitcast.69), calls=%async_computation.2 | async-start | bytes 2621440 | tf_op jit(solution)/shard_map/all_to_all | solution.py:185
  207.8 58.4 %psum.7 = f32[]{:T(128)} all-reduce(f32[]{:T(128)} %get-tuple-element.5), channel_id=1, replica_groups=mesh['ctx'=4,'rec'=8] {'ctx','rec'}, use_global_device_ids=true, to_apply=%region_18.19 | all-reduce | flops 1 | bytes 8 | tf_op jit(solution)/shard_map/psum | solution.py:179
  266.9 5.5 %gather_fusion.1 = bf16[512,1280]{1,0:T(8,128)(2,1)} fusion(bf16[512,1280]{1,0:T(8,128)(2,1)} %bitcast.70, s32[1024]{0:T(1024)S(1)} %pad_clamp_fusion), kind=kCustom, calls=%fused_computation.1 | custom fusion | bytes 2623488 | tf_op jit(solution)/shard_map/gather | solution.py:193
  272.5 2.5 broadcast_select_fusion
  275.0 91.2 %reduce-scatter.8.cloned.1.call-done = f32[40,1280]{1,0:T(8,128)} async-done(((f32[1280,1280]{1,0:T(8,128)}), f32[40,1280]{1,0:T(8,128)}) %reduce-scatter.8.cloned.1.call-update) | async-done | bytes 204816 | tf_op jit(solution)/shard_map/reduce_scatter | solution.py:169
  (207 shorter events, 82.7 us)
Async XLA Ops:
  7.2 116.0 %copy-start = (bf16[1280,1280]{1,0:T(8,128)(2,1)S(1)}, bf16[1280,1280]{1,0:T(8,128)(2,1)}, u32[]{:S(2)}) copy-start(bf16[1280,1280]{1,0:T(8,128)(2,1)} %param.12) | copy-start | bytes 9830404
  7.2 57.4 %all-gather.2.cloned.1.call-start = ((), (), s32[]{:S(2)}) async-start(), calls=%async_computation.6 | async-start | bytes 1638400 | tf_op jit(solution)/shard_map/all_gather | solution.py:150
  7.2 15.7 %collective-permute-start = (bf16[1,128,1280]{2,1,0:T(8,128)(2,1)}, bf16[1,128,1280]{2,1,0:T(8,128)(2,1)}, u32[]{:S(2)}, u32[]{:S(2)}) collective-permute-start(bf16[1,128,1280]{2,1,0:T(8,128)(2,1)} %param.11), channel_id=1, source_target_pairs={{0,8},{8,16},{16,24},{24,0},{1,9},{9,17},{17,25},{25,1},{2,10},{10... | collective-permute-start | bytes 983048 | tf_op jit(solution)/shard_map/ppermute | solution.py:17
  10.3 40.4 %collective-permute-start.2 = (bf16[1,128,1280]{2,1,0:T(8,128)(2,1)}, bf16[1,128,1280]{2,1,0:T(8,128)(2,1)}, u32[]{:S(2)}, u32[]{:S(2)}) collective-permute-start(bf16[1,128,1280]{2,1,0:T(8,128)(2,1)} %param.11), channel_id=1, source_target_pairs={{0,24},{8,0},{16,8},{24,16},{1,25},{9,1},{17,9},{25,17},{2,26},{10... | collective-permute-start | bytes 983048 | tf_op jit(solution)/shard_map/ppermute | solution.py:19
  13.1 2.3 copy-start.47
  15.4 9.3 %copy-start.46 = (s32[512]{0:T(512)}, s32[512]{0:T(512)S(1)}, u32[]{:S(2)}) copy-start(s32[512]{0:T(512)S(1)} %get-tuple-element.28) | copy-start | bytes 6148
  18.7 24.0 %all-to-all-start = ((s32[32,1,16]{2,1,0:T(1,128)}), s32[32,1,16]{2,1,0:T(1,128)S(1)}, u32[]{:S(2)}, u32[]{:S(2)}) async-start(s32[32,1,16]{2,1,0:T(1,128)} %bitcast.16), calls=%async_computation | async-start | bytes 32768 | tf_op jit(solution)/shard_map/all_to_all | solution.py:134
  22.9 24.7 %collective-permute-start.1 = (bf16[1,128,1280]{2,1,0:T(8,128)(2,1)}, bf16[1,128,1280]{2,1,0:T(8,128)(2,1)}, u32[]{:S(2)}, u32[]{:S(2)}) collective-permute-start(bf16[1,128,1280]{2,1,0:T(8,128)(2,1)} %collective-permute-done), channel_id=1, source_target_pairs={{0,8},{8,16},{16,24},{24,0},{1,9},{9,17},{17,25},{25,1},{2,10},{10... | collective-permute-start | bytes 983048 | tf_op jit(solution)/shard_map/ppermute | solution.py:17
  42.7 76.2 %all-to-all-start.1 = ((bf16[32,16,1280]{2,1,0:T(8,128)(2,1)}), bf16[32,16,1280]{2,1,0:T(8,128)(2,1)}, u32[]{:S(2)}, u32[]{:S(2)}) async-start(bf16[32,16,1280]{2,1,0:T(8,128)(2,1)} %bitcast.199), calls=%async_computation.1 | async-start | bytes 2621440 | tf_op jit(solution)/shard_map/all_to_all | solution.py:127
  46.1 229.0 %reduce-scatter.6.cloned.1.call-start = ((), (), s32[]{:S(2)}) async-start(), calls=%async_computation.8 | async-start | bytes 1638400 | tf_op jit(solution)/shard_map/reduce_scatter | solution.py:165
  47.6 6.1 %copy-start.15 = (bf16[1,128,1280]{2,1,0:T(8,128)(2,1)S(1)}, bf16[1,128,1280]{2,1,0:T(8,128)(2,1)}, u32[]{:S(2)}) copy-start(bf16[1,128,1280]{2,1,0:T(8,128)(2,1)} %param.11) | copy-start | bytes 983044
  70.9 3.3 copy-start.45
  70.9 2.9 copy-start.33
  70.9 5.9 %copy-start.40 = (bf16[256,256]{0,1:T(8,128)(2,1)S(1)}, bf16[256,256]{0,1:T(8,128)(2,1)}, u32[]{:S(2)}) copy-start(bf16[256,256]{0,1:T(8,128)(2,1)} %copy.94) | copy-start | bytes 393220
  74.2 7.5 %copy-start.16 = (bf16[4,64,256]{2,1,0:T(8,128)(2,1)}, bf16[4,64,256]{2,1,0:T(8,128)(2,1)S(1)}, u32[]{:S(2)}) copy-start(bf16[4,64,256]{2,1,0:T(8,128)(2,1)S(1)} %convolution_convert_fusion.8) | copy-start | bytes 393220
  79.8 3.3 copy-start.44
  79.8 2.9 copy-start.32
  79.8 5.9 %copy-start.38 = (bf16[256,256]{0,1:T(8,128)(2,1)S(1)}, bf16[256,256]{0,1:T(8,128)(2,1)}, u32[]{:S(2)}) copy-start(bf16[256,256]{0,1:T(8,128)(2,1)} %copy.103) | copy-start | bytes 393220
  83.2 7.5 %copy-start.22 = (bf16[4,64,256]{2,1,0:T(8,128)(2,1)}, bf16[4,64,256]{2,1,0:T(8,128)(2,1)S(1)}, u32[]{:S(2)}) copy-start(bf16[4,64,256]{2,1,0:T(8,128)(2,1)S(1)} %convolution_convert_fusion.9) | copy-start | bytes 393220
  88.9 2.9 copy-start.31
  88.9 5.9 %copy-start.36 = (bf16[256,256]{0,1:T(8,128)(2,1)S(1)}, bf16[256,256]{0,1:T(8,128)(2,1)}, u32[]{:S(2)}) copy-start(bf16[256,256]{0,1:T(8,128)(2,1)} %copy.107) | copy-start | bytes 393220
  92.2 7.5 %copy-start.19 = (bf16[4,64,256]{2,1,0:T(8,128)(2,1)}, bf16[4,64,256]{2,1,0:T(8,128)(2,1)S(1)}, u32[]{:S(2)}) copy-start(bf16[4,64,256]{2,1,0:T(8,128)(2,1)S(1)} %convolution_convert_fusion.7) | copy-start | bytes 393220
  97.8 2.9 copy-start.30
  106.9 2.8 copy-start.28
  126.3 2.5 copy-start.11
  126.3 3.8 %copy-start.17 = (bf16[4,64,256]{2,1,0:T(8,128)(2,1)S(1)}, bf16[4,64,256]{2,1,0:T(8,128)(2,1)}, u32[]{:S(2)}) copy-start(bf16[4,64,256]{2,1,0:T(8,128)(2,1)} %copy-done.16) | copy-start | bytes 393220
  127.0 3.8 %copy-start.3 = (bf16[4,256,512]{2,1,0:T(8,128)(2,1)S(1)}, bf16[4,256,512]{2,1,0:T(8,128)(2,1)}, u32[]{:S(2)}) copy-start(bf16[4,256,512]{2,1,0:T(8,128)(2,1)} %copy-done.2) | copy-start | bytes 3145732
  127.1 3.6 copy-start.18
  129.1 8.1 %copy-start.5 = (bf16[4,256,512]{2,1,0:T(8,128)(2,1)S(1)}, bf16[4,256,512]{2,1,0:T(8,128)(2,1)}, u32[]{:S(2)}) copy-start(bf16[4,256,512]{2,1,0:T(8,128)(2,1)} %copy-done.4) | copy-start | bytes 3145732
  130.8 9.5 %copy-start.7 = (bf16[4,256,512]{2,1,0:T(8,128)(2,1)S(1)}, bf16[4,256,512]{2,1,0:T(8,128)(2,1)}, u32[]{:S(2)}) copy-start(bf16[4,256,512]{2,1,0:T(8,128)(2,1)} %copy-done.6) | copy-start | bytes 3145732
  135.6 3.7 copy-start.21
  137.2 4.8 %copy-start.9 = (bf16[4,256,512]{2,1,0:T(8,128)(2,1)S(1)}, bf16[4,256,512]{2,1,0:T(8,128)(2,1)}, u32[]{:S(2)}) copy-start(bf16[4,256,512]{2,1,0:T(8,128)(2,1)} %copy-done.8) | copy-start | bytes 3145732
  140.3 3.9 %copy-start.25 = (bf16[512,256]{1,0:T(8,128)(2,1)S(1)}, bf16[512,256]{1,0:T(8,128)(2,1)}, u32[]{:S(2)}) copy-start(bf16[512,256]{1,0:T(8,128)(2,1)} %copy.126) | copy-start | bytes 786436
  143.0 4.4 %copy-start.14 = (f32[4,256,512]{2,1,0:T(8,128)S(1)}, f32[4,256,512]{2,1,0:T(8,128)}, u32[]{:S(2)}) copy-start(f32[4,256,512]{2,1,0:T(8,128)} %get-tuple-element.32) | copy-start | bytes 6291460
  147.3 127.7 %reduce-scatter.4.cloned.1.call-start = ((), (), s32[]{:S(2)}) async-start(), calls=%async_computation.7 | async-start | bytes 1638400 | tf_op jit(solution)/shard_map/reduce_scatter | solution.py:162
  150.0 2.2 copy-start.41
  153.4 2.3 copy-start.39
  159.5 3.3 copy-start.37
  165.6 3.2 copy-start.35
  168.8 4.5 %copy-start.24 = (bf16[512,256]{1,0:T(8,128)(2,1)S(1)}, bf16[512,256]{1,0:T(8,128)(2,1)}, u32[]{:S(2)}) copy-start(bf16[512,256]{1,0:T(8,128)(2,1)} %copy.121) | copy-start | bytes 786436
  171.6 5.9 %copy-start.26 = (bf16[512,256]{1,0:T(8,128)(2,1)S(1)}, bf16[512,256]{1,0:T(8,128)(2,1)}, u32[]{:S(2)}) copy-start(bf16[512,256]{1,0:T(8,128)(2,1)} %copy.124) | copy-start | bytes 786436
  178.3 187.9 %reduce-scatter.8.cloned.1.call-start = ((), (), s32[]{:S(2)}) async-start(), calls=%async_computation.9 | async-start | bytes 6758400 | tf_op jit(solution)/shard_map/reduce_scatter | solution.py:169
  186.7 8.1 %copy-start.27 = (bf16[512,256]{0,1:T(8,128)(2,1)S(1)}, bf16[512,256]{0,1:T(8,128)(2,1)}, u32[]{:S(2)}) copy-start(bf16[512,256]{0,1:T(8,128)(2,1)} %copy.100) | copy-start | bytes 786436
  194.8 2.1 copy-start.34
  199.9 7.9 %copy-start.43 = (s32[512]{0:T(512)S(1)}, s32[512]{0:T(512)}, u32[]{:S(2)}) copy-start(s32[512]{0:T(512)} %get-tuple-element.27) | copy-start | bytes 6148
  199.9 67.0 %all-to-all-start.2 = ((bf16[32,16,1280]{2,1,0:T(8,128)(2,1)}), bf16[32,16,1280]{2,1,0:T(8,128)(2,1)}, u32[]{:S(2)}, u32[]{:S(2)}) async-start(bf16[32,16,1280]{2,1,0:T(8,128)(2,1)} %bitcast.69), calls=%async_computation.2 | async-start | bytes 2621440 | tf_op jit(solution)/shard_map/all_to_all | solution.py:185
  266.9 5.6 %copy-start.48 = (pred[512]{0:T(512)(128)(4,1)S(1)}, pred[512]{0:T(512)(128)(4,1)}, u32[]{:S(2)}) copy-start(pred[512]{0:T(512)(128)(4,1)} %copy-done.47) | copy-start | bytes 1540
  266.9 99.3 %copy-start.1 = (bf16[1280,1280]{1,0:T(8,128)(2,1)S(1)}, bf16[1280,1280]{1,0:T(8,128)(2,1)}, u32[]{:S(2)}) copy-start(bf16[1280,1280]{1,0:T(8,128)(2,1)} %param.12) | copy-start | bytes 9830404
  (11 other events, 10.8 us)
Sparse Core Ops, SparseCore 0:
  12.5 51.9 all-gather.1
  147.4 34.2 reduce-scatter.5
  184.6 31.0 reduce-scatter.3
  218.4 147.7 reduce-scatter.7
